TPU v7x, 512 devices: a whole 4x4x16 slice. The times are simulated.
512 devices in a mesh: tm: 16 (over y, x_lo, core), chan: 32 (over z, x_hi).
Axes of the slice: x: 4 (x_hi: 2, x_lo: 2; x = x_hi * 2 + x_lo), y: 4, z: 16, core: 2. Of those that a mesh axis runs over, the one named last changes fastest.
Arguments:
- raw: bfloat16 [16384, 4096], P('tm', 'chan'), may hold values from -6 to 6
- taps: bfloat16 [512], replicated, may hold values from -0.25 to 0.25
Outputs:
- correlations: float32 [4096, 64, 1024], P('chan', 'tm')
All inputs are finite; a program needn't handle non-finite values.
Results may differ from a plain program's by a relative error of at most 0.0044.
Values may be sent and summed in bfloat16 or wider, within the bound.
No kernel may reach another device: no remote copies, remote signals or barrier semaphores. Data moves between devices by JAX's collectives and lax.ppermute only.
A program may use at most 128 MiB of HBM per device.

v0:
```python
import math
import jax
import jax.numpy as jnp
from jax import lax
from jax.sharding import PartitionSpec as P

TAPS = 512
HW = 64
FR = 1024
SRC_DEV = 2
LAGS = 1024
epsilon = 1e-05


def shifted(block, axis, distance):
    devices = range(lax.axis_size(axis))
    route = [(i - distance, i) for i in devices if i - distance in devices]
    return lax.ppermute(block, axis, route)


def padded(array, sides, width):
    for axis, dim in sides:
        count, length = (lax.axis_size(axis), array.shape[dim])
        up = [(i, (i + 1) % count) for i in range(count - 1)]
        down = [(j, i) for i, j in up]
        last = lax.slice_in_dim(array, length - width, length, axis=dim)
        initial = lax.slice_in_dim(array, 0, width, axis=dim)
        before = lax.ppermute(last, axis, up)
        after = lax.ppermute(initial, axis, down)
        array = jnp.concatenate([before, array, after], axis=dim)
    return array


def forward_table(first, count):
    freq = first + jnp.arange(count, dtype=jnp.int32)
    sample = jnp.arange(FR, dtype=jnp.int32)
    phase = freq[:, None] * sample[None, :] % (2 * FR)
    angle = phase.astype(jnp.float32) * (math.pi / FR)
    return jnp.stack([jnp.cos(angle), -jnp.sin(angle)])


def inverse_table(first, count, scale):
    freq = first + jnp.arange(count, dtype=jnp.int32)
    lagged = jnp.arange(LAGS, dtype=jnp.int32) - LAGS // 2 + 2 * FR
    phase = freq[:, None] * lagged[None, :] % (2 * FR)
    angle = phase.astype(jnp.float32) * (math.pi / FR)
    weight = jnp.where(freq == 0, 1.0, 2.0).astype(jnp.float32) * (scale / (2 * FR))
    return jnp.stack([weight[:, None] * jnp.cos(angle), -weight[:, None] * jnp.sin(angle)])


def transform(frames32, pattern, axis_out):
    width = min(256, FR)
    pieces = []
    for first in range(0, FR, width):
        table = forward_table(first, width)
        pieces.append(jnp.einsum(pattern, table, frames32, precision=lax.Precision.HIGHEST))
    return jnp.concatenate(pieces, axis_out)


def correlate(cross, scale):
    width = min(256, FR)
    result = jnp.zeros(cross.shape[:2] + (LAGS,), jnp.float32)
    for first in range(0, FR, width):
        table = inverse_table(first, width, scale)
        result = result + jnp.einsum(
            "rkgf,gfl->rkl",
            cross[..., first : first + width],
            table,
            precision=lax.Precision.HIGHEST,
        )
    return result


def on_device(raw, taps):
    samples, channels = raw.shape
    time_parts = lax.axis_size("tm")
    chan_parts = lax.axis_size("chan")
    frames_dev = samples // FR
    frame_total = frames_dev * time_parts
    sources_total = SRC_DEV * chan_parts
    stride = channels // SRC_DEV
    scale = 1.0 / math.sqrt(frame_total * FR)
    kernel = jnp.broadcast_to(taps[:, None, None], (TAPS, 1, channels))
    before = shifted(raw[samples - TAPS + 1 :], "tm", 1)
    filtered = lax.conv_general_dilated(
        jnp.concatenate([before, raw], 0)[None],
        kernel,
        (1,),
        "VALID",
        dimension_numbers=("NWC", "WIO", "NWC"),
        feature_group_count=channels,
        preferred_element_type=jnp.float32,
    )[0]
    widened = padded(filtered, (("tm", 0),), HW)
    total = lax.reduce_window(
        jnp.abs(widened), jnp.zeros((), jnp.float32), lax.add, (2 * HW + 1, 1), (1, 1), "VALID"
    )
    level = total / (2 * HW + 1)
    whitened = (widened[HW : HW + samples] / (level + epsilon)).astype(jnp.bfloat16)
    frames32 = whitened.astype(jnp.float32).reshape(frames_dev, FR, channels)
    spectra = transform(frames32, "gft,btc->bgfc", 2).astype(jnp.bfloat16)
    banded = lax.all_to_all(spectra, "tm", split_axis=2, concat_axis=0, tiled=True)
    own_re = banded[:, 0]
    own_im = banded[:, 1]
    picked = banded[..., ::stride]
    band_width = banded.shape[2]
    empty = jnp.zeros((channels, sources_total, 2, band_width), jnp.float32)
    piece = lax.all_gather(picked, "chan", axis=3, tiled=True)
    piece_re = piece[:, 0]
    piece_im = piece[:, 1]
    real_part = jnp.einsum(
        "bfs,bfc->csf", piece_re, own_re, preferred_element_type=jnp.float32
    ) + jnp.einsum("bfs,bfc->csf", piece_im, own_im, preferred_element_type=jnp.float32)
    imag_part = jnp.einsum(
        "bfs,bfc->csf", piece_re, own_im, preferred_element_type=jnp.float32
    ) - jnp.einsum("bfs,bfc->csf", piece_im, own_re, preferred_element_type=jnp.float32)
    stacked = jnp.stack([real_part, imag_part], 2)
    cross = lax.dynamic_update_slice_in_dim(empty, stacked, jnp.int32(0), 1)
    return correlate(lax.all_to_all(cross, "tm", split_axis=1, concat_axis=3, tiled=True), scale)


def solution(mesh):
    placed = (P("tm", "chan"), P())
    return jax.shard_map(
        on_device, mesh=mesh, in_specs=placed, out_specs=P("chan", "tm", None), check_vma=False
    )
```

profile of v0, /device:TPU:1, one launch (start us, length us, event | category | flops | bytes accessed | tf_op | source)
XLA Modules:
  0.0 304.3 jit_solution(13636452753575318065)
XLA Ops:
  0.0 1.0 slice.42
  1.0 4.5 %collective-permute-start = (bf16[511,128]{1,0:T(8,128)(2,1)S(1)}, bf16[511,128]{1,0:T(8,128)(2,1)S(1)}, u32[]{:S(2)}, u32[]{:S(2)}) collective-permute-start(bf16[511,128]{1,0:T(8,128)(2,1)S(1)} %slice.42), channel_id=1, source_target_pairs={{0,32},{32,64},{64,96},{96,128},{128,160},{160,192},{192,224},{224... | collective-permute-start | bytes 392456 | tf_op jit(solution)/shard_map/ppermute | solution.py:18
  5.6 0.0 copy-start.15
  5.6 32.5 %cosine_multiply_fusion = (f32[1,256,1024]{2,1,0:T(8,128)}, f32[1,256,1024]{2,1,0:T(8,128)}, f32[1,256,1024]{2,1,0:T(8,128)}, f32[1,256,1024]{2,1,0:T(8,128)}, f...) fusion(f32[256]{0:T(256)S(1)} %get-tuple-element.30, ...), kind=kLoop, calls=%fused_computation.105 | loop fusion | flops 28573696 | bytes 14695424 | tf_op jit(solution)/shard_map/mul | solution.py:48
  38.1 0.0 copy-done
  38.1 0.6 fusion.132
  38.7 0.0 collective-permute-done
  38.7 0.0 copy-done.15
  38.7 0.1 maximum_bitcast_fusion.10
  38.8 44.4 %fusion.95 = f32[1,1024,128]{2,0,1:T(1,128)S(1)} fusion(bf16[1,1535,128]{2,1,0:T(8,128)(2,1)S(1)} %maximum_bitcast_fusion.10, bf16[512,1,128]{2,1,0:T(2,128)(2,1)S(1)} %fusion.132), kind=kOutput, calls=%fused_computation.131 | convolution fusion | flops 134217728 | bytes 1048320 | tf_op jit(solution)/shard_map/conv_general_dilated | solution.py:85
  83.2 0.0 copy-start.14
  83.2 1.9 collective-permute-start.1
  85.1 4.9 %collective-permute-start.2 = (f32[64,128]{1,0:T(8,128)S(1)}, f32[64,128]{1,0:T(8,128)S(1)}, u32[]{:S(2)}, u32[]{:S(2)}) collective-permute-start(f32[64,128]{1,0:T(8,128)S(1)} %get-tuple-element.8), channel_id=1, source_target_pairs={{32,0},{64,32},{96,64},{128,96},{160,128},{192,160},{224,192},{256... | collective-permute-start | bytes 98312 | tf_op jit(solution)/shard_map/ppermute | solution.py:29
  90.1 4.1 %sine_negate_fusion.3 = (f32[1,256,1024]{2,1,0:T(8,128)S(1)}, f32[1,256,1024]{2,1,0:T(8,128)S(1)}) fusion(), kind=kLoop, calls=%fused_computation.123 | loop fusion | flops 3932160 | bytes 2097152 | tf_op jit(solution)/shard_map/neg | solution.py:39
  94.2 0.0 collective-permute-done.1
  94.2 0.0 collective-permute-done.2
  94.2 0.0 copy-done.14
  94.2 0.9 maximum_abs_fusion
  95.2 19.6 %reduce_window.7 = f32[1,1024,128]{2,1,0:T(8,128)} reduce-window(f32[1,1152,128]{2,1,0:T(8,128)} %maximum_abs_fusion, f32[]{:T(128)} %constant.65.clone.1), window={size=1x129x1}, to_apply=%region_0.0 | reduce-window | flops 16777216 | bytes 1114116 | tf_op jit(solution)/shard_map/reduce_window | solution.py:95
  114.8 1.4 divide_convert_fusion
  116.2 1.7 fusion.40
  118.0 1.3 fusion.46
  119.3 1.3 fusion.43
  120.6 1.3 fusion.49
  122.0 0.1 pad_maximum_fusion.1
  122.0 0.4 copy.91
  122.4 12.6 %all_to_all.36 = bf16[1,2,1024,128]{3,1,0,2:T(2,128)(2,1)S(1)} all-to-all(bf16[1,2,1024,128]{3,1,0,2:T(2,128)(2,1)S(1)} %copy.91), channel_id=1, replica_groups=mesh['tm'=16,'chan'=32] {'tm'}, dimensions={2} | all-to-all | bytes 1048576 | tf_op jit(solution)/shard_map/all_to_all | solution.py:102
  135.1 0.3 copy.128
  135.4 2.0 slice.48
  137.4 0.5 copy.94
  137.9 71.7 %all_gather.3 = bf16[16,2,64,64]{2,0,1,3:T(8,128)(2,1)S(1)} all-gather(bf16[16,2,64,2]{2,0,1,3:T(8,128)(2,1)S(1)} %copy.94), channel_id=1, replica_groups=mesh['tm'=16,'chan'=32] {'chan'}, dimensions={3}, use_global_device_ids=true | all-gather | bytes 270336 | tf_op jit(solution)/shard_map/all_gather | solution.py:108
  209.7 0.4 copy.118
  210.1 1.8 fusion.107
  211.9 0.5 fusion.109
  212.4 0.4 copy.119
  212.8 2.1 subtract_bitcast_fusion
  214.9 0.5 add_bitcast_fusion
  215.4 0.6 pad_maximum_fusion
  215.9 2.4 copy.97
  218.4 66.6 %all_to_all.37 = f32[128,64,2,64]{0,3,2,1:T(8,128)S(1)} all-to-all(f32[128,64,2,64]{0,3,2,1:T(8,128)S(1)} %copy.97), channel_id=1, replica_groups=mesh['tm'=16,'chan'=32] {'tm'}, dimensions={1} | all-to-all | bytes 8388608 | tf_op jit(solution)/shard_map/all_to_all | solution.py:119
  285.0 0.6 copy.98
  285.6 0.6 copy-done.5
  286.2 0.3 copy-done.6
  286.6 3.5 %fusion.22 = f32[128,4,1024,1]{2,0,3,1:T(8,128)S(1)} fusion(f32[1,256,1024]{2,1,0:T(8,128)S(1)} %copy-done.5, f32[1,256,1024]{2,1,0:T(8,128)S(1)} %copy-done.6, f32[128,4,2,1024]{0,3,2,1:T(8,128)S(1)} %bitcast.109), kind=kOutput, calls=%fused_computation.26 | convolution fusion | flops 3221749760 | bytes 5242880 | tf_op jit(solution)/shard_map/rkgf,gfl->rkl/dot_general | solution.py:65
  290.2 3.6 %fusion.19 = f32[128,4,1024,1]{2,0,3,1:T(8,128)S(1)} fusion(f32[1,256,1024]{2,1,0:T(8,128)S(1)} %copy-done.3, f32[1,256,1024]{2,1,0:T(8,128)S(1)} %copy-done.4, f32[128,4,2,1024]{0,3,2,1:T(8,128)S(1)} %bitcast.110), kind=kOutput, calls=%fused_computation.22 | convolution fusion | flops 3221749760 | bytes 5242880 | tf_op jit(solution)/shard_map/rkgf,gfl->rkl/dot_general | solution.py:65
  293.8 3.6 %fusion.16 = f32[128,4,1024,1]{2,0,3,1:T(8,128)S(1)} fusion(f32[1,256,1024]{2,1,0:T(8,128)S(1)} %copy-done.1, f32[1,256,1024]{2,1,0:T(8,128)S(1)} %copy-done.2, f32[128,4,2,1024]{0,3,2,1:T(8,128)S(1)} %bitcast.111), kind=kOutput, calls=%fused_computation.18 | convolution fusion | flops 3221749760 | bytes 5242880 | tf_op jit(solution)/shard_map/rkgf,gfl->rkl/dot_general | solution.py:65
  297.3 4.1 %bitcast_add_fusion = f32[128,4,1024]{2,0,1:T(8,128)S(1)} fusion(f32[128,4,1024,1]{2,0,3,1:T(8,128)S(1)} %fusion.22, f32[128,4,1024,1]{2,0,3,1:T(8,128)S(1)} %fusion.19, f32[128,4,1024,1]{2,0,3,1:T(8,128)S(1)} %fusion.16, f32[1,256,1024]{2,1,0:T(8,128)S(1)} %copy-done.13, f32[1,256,1024]{2,1,0:T(8,128)S(1)} %copy-done.12, f32[128,4,2,1024]{0,3,2,1:T(8,128)S(1)} %bitcast.112), kind=kOutput, calls=%fused_computation.33 | convolution fusion | flops 3223322624 | bytes 11534336 | tf_op jit(solution)/shard_map/rkgf,gfl->rkl/dot_general | solution.py:65
  301.4 2.7 copy.103
  (34 shorter events, 0.1 us)
Async XLA Ops:
  0.0 38.1 %copy-start = (bf16[512]{0:T(512)(128)(2,1)S(1)}, bf16[512]{0:T(512)(128)(2,1)}, u32[]{:S(2)}) copy-start(bf16[512]{0:T(512)(128)(2,1)} %param.3) | copy-start | bytes 3076
  1.0 37.7 %collective-permute-start = (bf16[511,128]{1,0:T(8,128)(2,1)S(1)}, bf16[511,128]{1,0:T(8,128)(2,1)S(1)}, u32[]{:S(2)}, u32[]{:S(2)}) collective-permute-start(bf16[511,128]{1,0:T(8,128)(2,1)S(1)} %slice.42), channel_id=1, source_target_pairs={{0,32},{32,64},{64,96},{96,128},{128,160},{160,192},{192,224},{224... | collective-permute-start | bytes 392456 | tf_op jit(solution)/shard_map/ppermute | solution.py:18
  5.6 33.1 %copy-start.15 = (bf16[1024,128]{1,0:T(8,128)(2,1)S(1)}, bf16[1024,128]{1,0:T(8,128)(2,1)}, u32[]{:S(2)}) copy-start(bf16[1024,128]{1,0:T(8,128)(2,1)} %param.2) | copy-start | bytes 786436
  83.2 11.0 %copy-start.14 = (f32[1,1024,128]{2,0,1:T(1,128)}, f32[1,1024,128]{2,0,1:T(1,128)S(1)}, u32[]{:S(2)}) copy-start(f32[1,1024,128]{2,0,1:T(1,128)S(1)} %fusion.95) | copy-start | bytes 1572868
  83.2 11.0 %collective-permute-start.1 = (f32[64,128]{1,0:T(8,128)S(1)}, f32[64,128]{1,0:T(8,128)S(1)}, u32[]{:S(2)}, u32[]{:S(2)}) collective-permute-start(f32[64,128]{1,0:T(8,128)S(1)} %get-tuple-element.7), channel_id=1, source_target_pairs={{0,32},{32,64},{64,96},{96,128},{128,160},{160,192},{192,224},{224... | collective-permute-start | bytes 98312 | tf_op jit(solution)/shard_map/ppermute | solution.py:28
  85.1 9.1 %collective-permute-start.2 = (f32[64,128]{1,0:T(8,128)S(1)}, f32[64,128]{1,0:T(8,128)S(1)}, u32[]{:S(2)}, u32[]{:S(2)}) collective-permute-start(f32[64,128]{1,0:T(8,128)S(1)} %get-tuple-element.8), channel_id=1, source_target_pairs={{32,0},{64,32},{96,64},{128,96},{160,128},{192,160},{224,192},{256... | collective-permute-start | bytes 98312 | tf_op jit(solution)/shard_map/ppermute | solution.py:29
  114.8 3.2 %copy-start.10 = (f32[1,256,1024]{2,1,0:T(8,128)S(1)}, f32[1,256,1024]{2,1,0:T(8,128)}, u32[]{:S(2)}) copy-start(f32[1,256,1024]{2,1,0:T(8,128)} %get-tuple-element.21) | copy-start | bytes 3145732
  114.8 3.2 %copy-start.11 = (f32[1,256,1024]{2,1,0:T(8,128)S(1)}, f32[1,256,1024]{2,1,0:T(8,128)}, u32[]{:S(2)}) copy-start(f32[1,256,1024]{2,1,0:T(8,128)} %get-tuple-element.22) | copy-start | bytes 3145732
  116.2 3.1 %copy-start.8 = (f32[1,256,1024]{2,1,0:T(8,128)S(1)}, f32[1,256,1024]{2,1,0:T(8,128)}, u32[]{:S(2)}) copy-start(f32[1,256,1024]{2,1,0:T(8,128)} %get-tuple-element.23) | copy-start | bytes 3145732
  116.2 3.1 %copy-start.9 = (f32[1,256,1024]{2,1,0:T(8,128)S(1)}, f32[1,256,1024]{2,1,0:T(8,128)}, u32[]{:S(2)}) copy-start(f32[1,256,1024]{2,1,0:T(8,128)} %get-tuple-element.24) | copy-start | bytes 3145732
  118.0 2.7 copy-start.7
  285.0 1.2 copy-start.5
  285.0 1.5 copy-start.6
  286.6 3.6 %copy-start.3 = (f32[1,256,1024]{2,1,0:T(8,128)S(1)}, f32[1,256,1024]{2,1,0:T(8,128)}, u32[]{:S(2)}) copy-start(f32[1,256,1024]{2,1,0:T(8,128)} %get-tuple-element.16) | copy-start | bytes 3145732
  286.6 3.6 %copy-start.4 = (f32[1,256,1024]{2,1,0:T(8,128)S(1)}, f32[1,256,1024]{2,1,0:T(8,128)}, u32[]{:S(2)}) copy-start(f32[1,256,1024]{2,1,0:T(8,128)} %get-tuple-element.17) | copy-start | bytes 3145732
  290.1 3.6 %copy-start.1 = (f32[1,256,1024]{2,1,0:T(8,128)S(1)}, f32[1,256,1024]{2,1,0:T(8,128)}, u32[]{:S(2)}) copy-start(f32[1,256,1024]{2,1,0:T(8,128)} %get-tuple-element.15) | copy-start | bytes 3145732
  290.1 3.6 %copy-start.2 = (f32[1,256,1024]{2,1,0:T(8,128)S(1)}, f32[1,256,1024]{2,1,0:T(8,128)}, u32[]{:S(2)}) copy-start(f32[1,256,1024]{2,1,0:T(8,128)} %get-tuple-element.20) | copy-start | bytes 3145732
  293.7 3.6 %copy-start.12 = (f32[1,256,1024]{2,1,0:T(8,128)S(1)}, f32[1,256,1024]{2,1,0:T(8,128)}, u32[]{:S(2)}) copy-start(f32[1,256,1024]{2,1,0:T(8,128)} %get-tuple-element.9) | copy-start | bytes 3145732
  293.7 3.6 %copy-start.13 = (f32[1,256,1024]{2,1,0:T(8,128)S(1)}, f32[1,256,1024]{2,1,0:T(8,128)}, u32[]{:S(2)}) copy-start(f32[1,256,1024]{2,1,0:T(8,128)} %get-tuple-element.10) | copy-start | bytes 3145732
where the time goes:
time: 307 us; the launch traced here: 304 us
  blocking collectives  151 us (49%)
  matrix products  69.7 us (23%)
  other arithmetic  59.3 us (19%)
  local copies, waits for them, and re-layouts  12.3 us (4%)
  starting transfers between devices  11.4 us (4%)
    all_gather x1, blocking collectives, on_device(): piece = lax.all_gather(picked, 'chan', axis=3, tiled=True)  71.7 us
    all_to_all x1, blocking collectives, on_device(): lax.all_to_all(cross, 'tm', split_axis=1, concat_axis=3, tiled=True)  66.6 us
    conv_general_dilated x1, matrix products, on_device(): lax.conv_general_dilated(jnp.concatenate([before, raw], 0)[None], kernel,...  44.4 us
    mul x1, other arithmetic, inverse_table(): weight[:, None] * jnp.cos(angle)  32.5 us
    another operation x1, other arithmetic, on_device(): lax.reduce_window(jnp.abs(widened), jnp.zeros((), jnp.float32), lax.add,...  19.6 us
    dot_general x4, matrix products, correlate(): jnp.einsum('rkgf,gfl->rkl', cross[..., first:first + width], table, preci...  14.8 us
    all_to_all x1, blocking collectives, on_device(): lax.all_to_all(spectra, 'tm', split_axis=2, concat_axis=0, tiled=True)  12.6 us
  transfers between devices with their start and end apart: 3, of which 0 were waited for; matrix products, arithmetic and copies ran while one was open for 12% of the time, Pallas kernels for 0%

commit v1 on v0

--- a/solution.py
+++ b/solution.py
@@ -105,7 +105,8 @@
     picked = banded[..., ::stride]
     band_width = banded.shape[2]
     empty = jnp.zeros((channels, sources_total, 2, band_width), jnp.float32)
-    piece = lax.all_gather(picked, "chan", axis=3, tiled=True)
+    outgoing = jnp.stack([picked] * lax.axis_size("chan"))
+    piece = jnp.concatenate(lax.all_to_all(outgoing, "chan", 0, 0), axis=3)
     piece_re = piece[:, 0]
     piece_im = piece[:, 1]
     real_part = jnp.einsum(

time: 307 us -> 262 us (0.85)
  blocking collectives: 151 us -> 105 us
    all_gather x1 -> x0, blocking collectives: 71.7 us -> none  [on_device(): piece = lax.all_gather(picked, 'chan', axis=3, tiled=True)]
    all_to_all x0 -> x1, blocking collectives: none -> 37.1 us  [on_device(): piece = jnp.concatenate(lax.all_to_all(outgoing, 'chan', 0, 0), axis=3)]
    all_to_all x1, blocking collectives: 66.6 us -> 54.9 us  [on_device(): lax.all_to_all(cross, 'tm', split_axis=1, concat_axis=3, tiled=True)]
  transfers between devices with their start and end apart: 3 -> 3, of which waited for: 0 -> 0; matrix products, arithmetic and copies ran while one was open for 12% -> 14% of each run, Pallas kernels for 0% -> 0%
where the time goes in v1:
time: 262 us; the launch traced here: 259 us
  blocking collectives  105 us (40%)
  matrix products  69.7 us (27%)
  other arithmetic  59.3 us (23%)
  local copies, waits for them, and re-layouts  13.2 us (5%)
  starting transfers between devices  11.4 us (4%)
    all_to_all x1, blocking collectives, on_device(): lax.all_to_all(cross, 'tm', split_axis=1, concat_axis=3, tiled=True)  54.9 us
    conv_general_dilated x1, matrix products, on_device(): lax.conv_general_dilated(jnp.concatenate([before, raw], 0)[None], kernel,...  44.4 us
    all_to_all x1, blocking collectives, on_device(): piece = jnp.concatenate(lax.all_to_all(outgoing, 'chan', 0, 0), axis=3)  37.1 us
    mul x1, other arithmetic, inverse_table(): weight[:, None] * jnp.cos(angle)  32.5 us
    another operation x1, other arithmetic, on_device(): lax.reduce_window(jnp.abs(widened), jnp.zeros((), jnp.float32), lax.add,...  19.6 us
    dot_general x4, matrix products, correlate(): jnp.einsum('rkgf,gfl->rkl', cross[..., first:first + width], table, preci...  14.8 us
    all_to_all x1, blocking collectives, on_device(): lax.all_to_all(spectra, 'tm', split_axis=2, concat_axis=0, tiled=True)  12.6 us
    dot_general x4, matrix products, transform(): jnp.einsum(pattern, table, frames32, precision=lax.Precision.HIGHEST)  5.64 us
  transfers between devices with their start and end apart: 3, of which 0 were waited for; matrix products, arithmetic and copies ran while one was open for 14% of the time, Pallas kernels for 0%

profile of v1, /device:TPU:1, one launch (start us, length us, event | category | flops | bytes accessed | tf_op | source)
XLA Modules:
  0.0 258.9 jit_solution(16370361623956535040)
XLA Ops:
  0.0 1.0 slice.42
  1.0 4.5 %collective-permute-start = (bf16[511,128]{1,0:T(8,128)(2,1)S(1)}, bf16[511,128]{1,0:T(8,128)(2,1)S(1)}, u32[]{:S(2)}, u32[]{:S(2)}) collective-permute-start(bf16[511,128]{1,0:T(8,128)(2,1)S(1)} %slice.42), channel_id=1, source_target_pairs={{0,32},{32,64},{64,96},{96,128},{128,160},{160,192},{192,224},{224... | collective-permute-start | bytes 392456 | tf_op jit(solution)/shard_map/ppermute | solution.py:18
  5.6 0.0 copy-start.15
  5.6 32.5 %cosine_multiply_fusion = (f32[1,256,1024]{2,1,0:T(8,128)}, f32[1,256,1024]{2,1,0:T(8,128)}, f32[1,256,1024]{2,1,0:T(8,128)}, f32[1,256,1024]{2,1,0:T(8,128)}, f...) fusion(f32[256]{0:T(256)S(1)} %get-tuple-element.30, ...), kind=kLoop, calls=%fused_computation.105 | loop fusion | flops 28573696 | bytes 14695424 | tf_op jit(solution)/shard_map/mul | solution.py:48
  38.1 0.0 copy-done
  38.1 0.6 fusion.132
  38.7 0.0 collective-permute-done
  38.7 0.1 maximum_bitcast_fusion.10
  38.8 44.4 %fusion.95 = f32[1,1024,128]{2,0,1:T(1,128)S(1)} fusion(bf16[1,1535,128]{2,1,0:T(8,128)(2,1)S(1)} %maximum_bitcast_fusion.10, bf16[512,1,128]{2,1,0:T(2,128)(2,1)S(1)} %fusion.132), kind=kOutput, calls=%fused_computation.131 | convolution fusion | flops 134217728 | bytes 1048320 | tf_op jit(solution)/shard_map/conv_general_dilated | solution.py:85
  83.2 1.9 collective-permute-start.1
  85.1 4.9 %collective-permute-start.2 = (f32[64,128]{1,0:T(8,128)S(1)}, f32[64,128]{1,0:T(8,128)S(1)}, u32[]{:S(2)}, u32[]{:S(2)}) collective-permute-start(f32[64,128]{1,0:T(8,128)S(1)} %get-tuple-element.8), channel_id=1, source_target_pairs={{32,0},{64,32},{96,64},{128,96},{160,128},{192,160},{224,192},{256... | collective-permute-start | bytes 98312 | tf_op jit(solution)/shard_map/ppermute | solution.py:29
  90.1 4.1 %sine_negate_fusion.3 = (f32[1,256,1024]{2,1,0:T(8,128)S(1)}, f32[1,256,1024]{2,1,0:T(8,128)S(1)}) fusion(), kind=kLoop, calls=%fused_computation.123 | loop fusion | flops 3932160 | bytes 2097152 | tf_op jit(solution)/shard_map/neg | solution.py:39
  94.2 0.0 collective-permute-done.1
  94.2 0.0 collective-permute-done.2
  94.2 0.9 maximum_abs_fusion
  95.2 19.6 %reduce_window.7 = f32[1,1024,128]{2,1,0:T(8,128)} reduce-window(f32[1,1152,128]{2,1,0:T(8,128)} %maximum_abs_fusion, f32[]{:T(128)} %constant.65.clone.1), window={size=1x129x1}, to_apply=%region_0.0 | reduce-window | flops 16777216 | bytes 1114116 | tf_op jit(solution)/shard_map/reduce_window | solution.py:95
  114.8 1.4 divide_convert_fusion
  116.2 1.7 fusion.40
  118.0 1.3 fusion.46
  119.3 1.3 fusion.43
  120.6 1.3 fusion.49
  122.0 0.1 pad_maximum_fusion.1
  122.0 0.4 copy.96
  122.4 12.6 %all_to_all.41 = bf16[1,2,1024,128]{3,1,0,2:T(2,128)(2,1)S(1)} all-to-all(bf16[1,2,1024,128]{3,1,0,2:T(2,128)(2,1)S(1)} %copy.96), channel_id=1, replica_groups=mesh['tm'=16,'chan'=32] {'tm'}, dimensions={2} | all-to-all | bytes 1048576 | tf_op jit(solution)/shard_map/all_to_all | solution.py:102
  135.1 0.3 copy.134
  135.4 2.0 slice.48
  137.4 0.5 copy.99
  137.9 0.1 broadcast_bitcast_fusion
  138.0 0.4 reshape.1217
  138.4 37.1 %all_to_all.42 = bf16[32,2,2048]{2,1,0:T(2,128)(2,1)S(1)} all-to-all(bf16[32,2,2048]{2,1,0:T(2,128)(2,1)S(1)} %reshape.1217), channel_id=1, replica_groups=mesh['tm'=16,'chan'=32] {'chan'}, dimensions={0} | all-to-all | bytes 524288 | tf_op jit(solution)/shard_map/all_to_all | solution.py:109
  175.5 0.4 reshape.1218
  176.0 0.4 copy.124
  176.4 1.8 fusion.107
  178.2 0.5 fusion.109
  178.7 0.4 copy.125
  179.1 2.1 subtract_bitcast_fusion
  181.2 0.5 add_bitcast_fusion
  181.7 0.6 pad_maximum_fusion
  182.2 2.4 copy.103
  184.7 54.9 %all_to_all.43 = f32[128,64,2,64]{0,3,2,1:T(8,128)S(1)} all-to-all(f32[128,64,2,64]{0,3,2,1:T(8,128)S(1)} %copy.103), channel_id=1, replica_groups=mesh['tm'=16,'chan'=32] {'tm'}, dimensions={1} | all-to-all | bytes 8388608 | tf_op jit(solution)/shard_map/all_to_all | solution.py:120
  239.5 0.6 copy.104
  240.1 0.6 copy-done.5
  240.8 0.3 copy-done.6
  241.1 3.5 %fusion.22 = f32[128,4,1024,1]{2,0,3,1:T(8,128)S(1)} fusion(f32[1,256,1024]{2,1,0:T(8,128)S(1)} %copy-done.5, f32[1,256,1024]{2,1,0:T(8,128)S(1)} %copy-done.6, f32[128,4,2,1024]{0,3,2,1:T(8,128)S(1)} %bitcast.115), kind=kOutput, calls=%fused_computation.26 | convolution fusion | flops 3221749760 | bytes 5242880 | tf_op jit(solution)/shard_map/rkgf,gfl->rkl/dot_general | solution.py:65
  244.7 3.6 %fusion.19 = f32[128,4,1024,1]{2,0,3,1:T(8,128)S(1)} fusion(f32[1,256,1024]{2,1,0:T(8,128)S(1)} %copy-done.3, f32[1,256,1024]{2,1,0:T(8,128)S(1)} %copy-done.4, f32[128,4,2,1024]{0,3,2,1:T(8,128)S(1)} %bitcast.116), kind=kOutput, calls=%fused_computation.22 | convolution fusion | flops 3221749760 | bytes 5242880 | tf_op jit(solution)/shard_map/rkgf,gfl->rkl/dot_general | solution.py:65
  248.3 3.6 %fusion.16 = f32[128,4,1024,1]{2,0,3,1:T(8,128)S(1)} fusion(f32[1,256,1024]{2,1,0:T(8,128)S(1)} %copy-done.1, f32[1,256,1024]{2,1,0:T(8,128)S(1)} %copy-done.2, f32[128,4,2,1024]{0,3,2,1:T(8,128)S(1)} %bitcast.117), kind=kOutput, calls=%fused_computation.18 | convolution fusion | flops 3221749760 | bytes 5242880 | tf_op jit(solution)/shard_map/rkgf,gfl->rkl/dot_general | solution.py:65
  251.9 4.1 %bitcast_add_fusion = f32[128,4,1024]{2,0,1:T(8,128)S(1)} fusion(f32[128,4,1024,1]{2,0,3,1:T(8,128)S(1)} %fusion.22, f32[128,4,1024,1]{2,0,3,1:T(8,128)S(1)} %fusion.19, f32[128,4,1024,1]{2,0,3,1:T(8,128)S(1)} %fusion.16, f32[1,256,1024]{2,1,0:T(8,128)S(1)} %copy-done.13, f32[1,256,1024]{2,1,0:T(8,128)S(1)} %copy-done.12, f32[128,4,2,1024]{0,3,2,1:T(8,128)S(1)} %bitcast.118), kind=kOutput, calls=%fused_computation.33 | convolution fusion | flops 3223322624 | bytes 11534336 | tf_op jit(solution)/shard_map/rkgf,gfl->rkl/dot_general | solution.py:65
  256.0 2.7 %copy.109 = f32[128,4,1024]{2,1,0:T(4,128)} copy(f32[128,4,1024]{2,0,1:T(8,128)S(1)} %bitcast_add_fusion) | data formatting | bytes 4194304 | tf_op jit(solution)/shard_map/add | solution.py:65
  (38 shorter events, 0.2 us)
Async XLA Ops:
  0.0 38.1 %copy-start = (bf16[512]{0:T(512)(128)(2,1)S(1)}, bf16[512]{0:T(512)(128)(2,1)}, u32[]{:S(2)}) copy-start(bf16[512]{0:T(512)(128)(2,1)} %param.3) | copy-start | bytes 3076
  1.0 37.7 %collective-permute-start = (bf16[511,128]{1,0:T(8,128)(2,1)S(1)}, bf16[511,128]{1,0:T(8,128)(2,1)S(1)}, u32[]{:S(2)}, u32[]{:S(2)}) collective-permute-start(bf16[511,128]{1,0:T(8,128)(2,1)S(1)} %slice.42), channel_id=1, source_target_pairs={{0,32},{32,64},{64,96},{96,128},{128,160},{160,192},{192,224},{224... | collective-permute-start | bytes 392456 | tf_op jit(solution)/shard_map/ppermute | solution.py:18
  5.6 33.1 %copy-start.15 = (bf16[1024,128]{1,0:T(8,128)(2,1)S(1)}, bf16[1024,128]{1,0:T(8,128)(2,1)}, u32[]{:S(2)}) copy-start(bf16[1024,128]{1,0:T(8,128)(2,1)} %param.2) | copy-start | bytes 786436
  83.2 11.0 %copy-start.14 = (f32[1,1024,128]{2,0,1:T(1,128)}, f32[1,1024,128]{2,0,1:T(1,128)S(1)}, u32[]{:S(2)}) copy-start(f32[1,1024,128]{2,0,1:T(1,128)S(1)} %fusion.95) | copy-start | bytes 1572868
  83.2 11.0 %collective-permute-start.1 = (f32[64,128]{1,0:T(8,128)S(1)}, f32[64,128]{1,0:T(8,128)S(1)}, u32[]{:S(2)}, u32[]{:S(2)}) collective-permute-start(f32[64,128]{1,0:T(8,128)S(1)} %get-tuple-element.7), channel_id=1, source_target_pairs={{0,32},{32,64},{64,96},{96,128},{128,160},{160,192},{192,224},{224... | collective-permute-start | bytes 98312 | tf_op jit(solution)/shard_map/ppermute | solution.py:28
  85.1 9.1 %collective-permute-start.2 = (f32[64,128]{1,0:T(8,128)S(1)}, f32[64,128]{1,0:T(8,128)S(1)}, u32[]{:S(2)}, u32[]{:S(2)}) collective-permute-start(f32[64,128]{1,0:T(8,128)S(1)} %get-tuple-element.8), channel_id=1, source_target_pairs={{32,0},{64,32},{96,64},{128,96},{160,128},{192,160},{224,192},{256... | collective-permute-start | bytes 98312 | tf_op jit(solution)/shard_map/ppermute | solution.py:29
  114.8 3.2 %copy-start.10 = (f32[1,256,1024]{2,1,0:T(8,128)S(1)}, f32[1,256,1024]{2,1,0:T(8,128)}, u32[]{:S(2)}) copy-start(f32[1,256,1024]{2,1,0:T(8,128)} %get-tuple-element.21) | copy-start | bytes 3145732
  114.8 3.2 %copy-start.11 = (f32[1,256,1024]{2,1,0:T(8,128)S(1)}, f32[1,256,1024]{2,1,0:T(8,128)}, u32[]{:S(2)}) copy-start(f32[1,256,1024]{2,1,0:T(8,128)} %get-tuple-element.22) | copy-start | bytes 3145732
  116.2 3.1 %copy-start.8 = (f32[1,256,1024]{2,1,0:T(8,128)S(1)}, f32[1,256,1024]{2,1,0:T(8,128)}, u32[]{:S(2)}) copy-start(f32[1,256,1024]{2,1,0:T(8,128)} %get-tuple-element.23) | copy-start | bytes 3145732
  116.2 3.1 %copy-start.9 = (f32[1,256,1024]{2,1,0:T(8,128)S(1)}, f32[1,256,1024]{2,1,0:T(8,128)}, u32[]{:S(2)}) copy-start(f32[1,256,1024]{2,1,0:T(8,128)} %get-tuple-element.24) | copy-start | bytes 3145732
  118.0 2.7 %copy-start.7 = (f32[1,256,1024]{2,1,0:T(8,128)S(1)}, f32[1,256,1024]{2,1,0:T(8,128)}, u32[]{:S(2)}) copy-start(f32[1,256,1024]{2,1,0:T(8,128)} %get-tuple-element.26) | copy-start | bytes 3145732
  239.5 1.2 copy-start.5
  239.5 1.5 copy-start.6
  241.1 3.6 %copy-start.3 = (f32[1,256,1024]{2,1,0:T(8,128)S(1)}, f32[1,256,1024]{2,1,0:T(8,128)}, u32[]{:S(2)}) copy-start(f32[1,256,1024]{2,1,0:T(8,128)} %get-tuple-element.16) | copy-start | bytes 3145732
  241.1 3.6 %copy-start.4 = (f32[1,256,1024]{2,1,0:T(8,128)S(1)}, f32[1,256,1024]{2,1,0:T(8,128)}, u32[]{:S(2)}) copy-start(f32[1,256,1024]{2,1,0:T(8,128)} %get-tuple-element.17) | copy-start | bytes 3145732
  244.7 3.6 %copy-start.1 = (f32[1,256,1024]{2,1,0:T(8,128)S(1)}, f32[1,256,1024]{2,1,0:T(8,128)}, u32[]{:S(2)}) copy-start(f32[1,256,1024]{2,1,0:T(8,128)} %get-tuple-element.15) | copy-start | bytes 3145732
  244.7 3.6 %copy-start.2 = (f32[1,256,1024]{2,1,0:T(8,128)S(1)}, f32[1,256,1024]{2,1,0:T(8,128)}, u32[]{:S(2)}) copy-start(f32[1,256,1024]{2,1,0:T(8,128)} %get-tuple-element.20) | copy-start | bytes 3145732
  248.3 3.6 %copy-start.12 = (f32[1,256,1024]{2,1,0:T(8,128)S(1)}, f32[1,256,1024]{2,1,0:T(8,128)}, u32[]{:S(2)}) copy-start(f32[1,256,1024]{2,1,0:T(8,128)} %get-tuple-element.9) | copy-start | bytes 3145732
  248.3 3.6 %copy-start.13 = (f32[1,256,1024]{2,1,0:T(8,128)S(1)}, f32[1,256,1024]{2,1,0:T(8,128)}, u32[]{:S(2)}) copy-start(f32[1,256,1024]{2,1,0:T(8,128)} %get-tuple-element.10) | copy-start | bytes 3145732
